TPU v7x, 128 devices: a whole 4x4x4 slice. The times are simulated.
128 devices in a mesh: layer: 4 (over x), row: 16 (over z, y), col: 2 (over core).
Axes of the slice: x: 4, y: 4, z: 4, core: 2. Of those that a mesh axis runs over, the one named last changes fastest.
Arguments:
- density: bfloat16 [8192, 8192], P('row', 'col'), may hold values from -0.5 to 1.5
- pattern: int32 [64, 64], P('row', 'col'), may hold values from 0 to 1, as said below
- holder: int32 [4096, 1], P(('layer', 'row', 'col')), may hold values from 0 to 31; in each aligned block of 32 rows (0 to 31, 32 to 63, ...) at most 2 rows name the same one
- slot_index: int32 [4096], P(('layer', 'row', 'col')), may hold values from 0 to 31
- atom_index: int32 [4096], P(('layer', 'row', 'col')), may hold values from 0 to 7
- derivative: bfloat16 [4096, 3, 128, 128], P(('layer', 'row', 'col')), may hold values from -1.1953125 to 1.1953125
Outputs:
- forces: float32 [3, 1024], P(None, ('layer', 'row', 'col'))
Inputs may be any that keep to these rules, and one draw needn't show every extreme that they name: `pattern`: the blocks held by one (row, col) grid position form a tile of 4 x 32; in some tile every block is 1. Among the derivative blocks of one device no holder is named more than 2 times, a bound that some block reaches; every holder is named on some device.
All inputs are finite; a program needn't handle non-finite values.
Results may differ from a plain program's by a relative error of at most 0.015.
Values may be sent and summed in bfloat16 or wider, within the bound.
A program may use at most 128 MiB of HBM per device.

v0:
```python
import jax
import jax.numpy as jnp
from jax import lax
from jax.sharding import PartitionSpec as P

BS = 128
ATOM_DEV = 8


def in_order(parts, dim):
    parts = jnp.moveaxis(parts, 0, dim)
    shape = parts.shape
    return parts.reshape(*shape[:dim], shape[dim] * shape[dim + 1], *shape[dim + 2 :])


def copy_for_each(value, axis):
    length = lax.axis_size(axis)
    return lax.all_to_all(
        jnp.broadcast_to(value[None], (length, *value.shape)), axis, 0, 0, tiled=True
    )


def gathered_copies(value, axis, dim):
    return in_order(copy_for_each(value, axis), dim)


def block_filter(matrix, kept_blocks):
    count_rows, count_cols = kept_blocks.shape
    blocked = matrix.reshape(count_rows, BS, count_cols, BS)
    return jnp.where(kept_blocks[:, None, :, None], blocked, jnp.zeros_like(blocked)).reshape(
        matrix.shape
    )


def column_subset(matrix, layer_count, layer_id):
    reshaped = matrix.reshape(matrix.shape[0], -1, layer_count, BS)
    picked = lax.dynamic_index_in_dim(reshaped, layer_id, 2, keepdims=False)
    return picked.reshape(matrix.shape[0], -1)


def row_subset(matrix, layer_count, layer_id):
    reshaped = matrix.reshape(-1, layer_count, BS, matrix.shape[1])
    picked = lax.dynamic_index_in_dim(reshaped, layer_id, 1, keepdims=False)
    return picked.reshape(-1, matrix.shape[1])


def multiply(left_matrix, right_matrix, layer_count, layer_id):
    left_part = column_subset(left_matrix, layer_count, layer_id)
    right_part = row_subset(right_matrix, layer_count, layer_id)
    row_strip = lax.all_gather(right_part, "row", axis=0, tiled=True)
    return jnp.dot(
        gathered_copies(left_part, "col", 1), row_strip, preferred_element_type=jnp.float32
    )


def shards(density, pattern, holder, slot_index, atom_index, derivative):
    layer_count = lax.axis_size("layer")
    layer_id = lax.axis_index("layer")
    grid_row = lax.axis_index("row")
    grid_col = lax.axis_index("col")
    row_blocks, col_blocks = pattern.shape
    global_rows = grid_row * row_blocks + jnp.arange(row_blocks, dtype=jnp.int32)
    global_cols = grid_col * col_blocks + jnp.arange(col_blocks, dtype=jnp.int32)
    kept_blocks = (pattern == 1) | (global_rows[:, None] == global_cols[None, :])
    filtered = block_filter(density, kept_blocks)
    partial_square = multiply(filtered, filtered, layer_count, layer_id)
    share_blocks = row_blocks // layer_count
    square_share = lax.psum_scatter(
        partial_square, "layer", scatter_dimension=0, tiled=True
    ).astype(jnp.bfloat16)
    square = lax.all_gather(square_share, "layer", axis=0, tiled=True)
    partial_cube = multiply(square, filtered, layer_count, layer_id)
    cube_share = lax.psum_scatter(partial_cube, "layer", scatter_dimension=0, tiled=True)
    kept_share = lax.dynamic_slice_in_dim(kept_blocks, layer_id * share_blocks, share_blocks, 0)
    purified = block_filter(
        3.0 * square_share.astype(jnp.float32) - 2.0 * cube_share, kept_share
    ).astype(jnp.bfloat16)
    held_blocks = (
        purified.reshape(share_blocks, BS, col_blocks, BS)
        .transpose(0, 2, 1, 3)
        .reshape(share_blocks * col_blocks, BS, BS)
    )
    holders_total = lax.axis_size("row") * lax.axis_size("col")
    entry_count = slot_index.shape[0]
    capacity = max(2, 2 * entry_count // holders_total)
    targets = holder[:, 0]
    target_hot = (targets[:, None] == jnp.arange(holders_total, dtype=jnp.int32)[None, :]).astype(
        jnp.int32
    )
    rank_values = jnp.sum(target_hot * (jnp.cumsum(target_hot, axis=0) - 1), axis=1)
    positions = targets * capacity + rank_values
    position_hot = (
        positions[None, :] == jnp.arange(holders_total * capacity, dtype=jnp.int32)[:, None]
    )
    requests = jnp.sum(jnp.where(position_hot, slot_index[None, :], 0), axis=1).reshape(
        holders_total, capacity
    )
    fetched = jnp.take(
        held_blocks,
        lax.all_to_all(requests, ("row", "col"), split_axis=0, concat_axis=0, tiled=True),
        axis=0,
    )
    returned = lax.all_to_all(fetched, ("row", "col"), split_axis=0, concat_axis=0, tiled=True)
    arrived = jnp.take(returned.reshape(holders_total * capacity, BS, BS), positions, axis=0)
    contrib = jnp.einsum("eij,exij->xe", arrived, derivative, preferred_element_type=jnp.float32)
    atom_hot = (atom_index[:, None] == jnp.arange(ATOM_DEV, dtype=jnp.int32)[None, :]).astype(
        jnp.float32
    )
    return -2.0 * jnp.dot(contrib, atom_hot, precision=lax.Precision.HIGHEST)


def solution(mesh):
    return jax.shard_map(
        shards,
        mesh=mesh,
        in_specs=(
            P("row", "col"),
            P("row", "col"),
            P(("layer", "row", "col"), None),
            P(("layer", "row", "col")),
            P(("layer", "row", "col")),
            P(("layer", "row", "col"), None, None, None),
        ),
        out_specs=P(None, ("layer", "row", "col")),
        check_vma=False,
    )
```

profile of v0, /device:TPU:0, one launch (start us, length us, event | category | flops | bytes accessed | tf_op | source)
XLA Modules:
  0.0 459.0 jit_solution(10009303842181600829)
XLA Ops:
  6.5 0.9 compare_or_fusion
  7.6 2.3 dynamic-slice_select_fusion
  10.1 6.5 %copy.40 = bf16[512,4096]{0,1:T(8,128)(2,1)} copy(bf16[512,4096]{1,0:T(8,128)(2,1)} %param.6) | data formatting | bytes 8388608 | tf_op args[0]
  16.7 1.3 dynamic-slice_select_fusion.1
  18.2 6.4 %all_to_all.30 = bf16[2,512,1024]{1,2,0:T(8,128)(2,1)} all-to-all(bf16[2,512,1024]{1,2,0:T(8,128)(2,1)S(1)} %broadcast_in_dim.109), channel_id=1, replica_groups=mesh['layer'=4,'row'=16,'col'=2] {'col'}, dimensions={0} | all-to-all | bytes 4194304 | tf_op jit(solution)/shard_map/all_to_all | solution.py:18
  24.6 99.4 %all-gather.6.cloned.1.call-done = bf16[1,1,2048,4096]{3,2,1,0:T(8,128)(2,1)} async-done(((bf16[1,1,128,4096]{3,2,1,0:T(8,128)(2,1)}), bf16[1,1,2048,4096]{3,2,1,0:T(8,128)(2,1)}) %all-gather.6.cloned.1.call-update) | async-done | bytes 16777232 | tf_op jit(solution)/shard_map/all_gather | solution.py:50
  124.0 15.1 %fusion.2 = f32[512,4096]{1,0:T(8,128)} fusion(bf16[512,2048]{0,1:T(8,128)(2,1)} %bitcast.69, bf16[1,1,2048,4096]{3,2,1,0:T(8,128)(2,1)} %all-gather.6.cloned.1.call-done), kind=kOutput, calls=%fused_computation.4 | convolution fusion | flops 8589934592 | bytes 27262976 | tf_op jit(solution)/shard_map/dot_general | solution.py:51
  139.2 80.1 %reduce-scatter.3.cloned.1.call-done = f32[128,4096]{1,0:T(8,128)} async-done(((f32[512,4096]{1,0:T(8,128)}), f32[128,4096]{1,0:T(8,128)}) %reduce-scatter.3.cloned.1.call-update) | async-done | bytes 2097168 | tf_op jit(solution)/shard_map/reduce_scatter | solution.py:68
  219.4 2.7 convert_element_type.14
  222.1 48.1 %all-gather.4.cloned.1.call-done = bf16[512,4096]{1,0:T(8,128)(2,1)} async-done(((bf16[128,4096]{1,0:T(8,128)(2,1)}), bf16[512,4096]{1,0:T(8,128)(2,1)}) %all-gather.4.cloned.1.call-update) | async-done | bytes 4194320 | tf_op jit(solution)/shard_map/all_gather | solution.py:71
  270.2 7.8 %reshape.121 = bf16[512,8,4,128]{3,2,1,0:T(4,128)(2,1)} reshape(bf16[512,4096]{1,0:T(8,128)(2,1)} %all-gather.4.cloned.1.call-done) | data formatting | bytes 8388608 | tf_op jit(solution)/shard_map/reshape | solution.py:36
  278.0 5.7 %constant_dynamic-slice_fusion = bf16[512,8,1,128]{3,2,1,0:T(2,128)(2,1)} fusion(bf16[512,8,4,128]{3,2,1,0:T(4,128)(2,1)} %reshape.121, s32[]{:T(128)S(6)} %select_n.68), kind=kLoop, calls=%fused_computation.36 | loop fusion | bytes 2097156 | tf_op jit(solution)/shard_map/jit(dynamic_index_in_dim)/dynamic_slice | solution.py:37
  283.7 5.8 %copy.48 = bf16[512,8,1,128]{0,3,1,2:T(8,128)(2,1)} copy(bf16[512,8,1,128]{3,2,1,0:T(2,128)(2,1)} %constant_dynamic-slice_fusion) | data formatting | bytes 2097152
  289.5 1.4 broadcast_in_dim.115
  290.9 5.4 %all_to_all.31 = bf16[2,512,1024]{1,2,0:T(8,128)(2,1)S(1)} all-to-all(bf16[2,512,1024]{1,2,0:T(8,128)(2,1)S(1)} %broadcast_in_dim.115), channel_id=1, replica_groups=mesh['layer'=4,'row'=16,'col'=2] {'col'}, dimensions={0} | all-to-all | bytes 4194304 | tf_op jit(solution)/shard_map/all_to_all | solution.py:18
  296.3 14.5 %fusion = f32[512,4096]{1,0:T(8,128)} fusion(bf16[512,2048]{0,1:T(8,128)(2,1)S(1)} %bitcast.70, bf16[1,1,2048,4096]{3,2,1,0:T(8,128)(2,1)} %all-gather.6.cloned.1.call-done), kind=kOutput, calls=%fused_computation.2 | convolution fusion | flops 8589934592 | bytes 27262976 | tf_op jit(solution)/shard_map/dot_general | solution.py:51
  310.9 0.6 copy-done.1
  311.9 0.7 all_to_all.19
  312.6 7.3 %all-to-all-start = ((s32[32,1,2]{2,1,0:T(1,128)}), s32[32,1,2]{2,1,0:T(1,128)S(1)}, u32[]{:S(2)}, u32[]{:S(2)}) async-start(s32[32,1,2]{2,1,0:T(1,128)} %bitcast.3), calls=%async_computation | async-start | bytes 32768 | tf_op jit(solution)/shard_map/all_to_all | solution.py:100
  320.0 7.3 %all-to-all-done = s32[32,1,2]{2,1,0:T(1,128)S(1)} async-done(((s32[32,1,2]{2,1,0:T(1,128)}), s32[32,1,2]{2,1,0:T(1,128)S(1)}, u32[]{:S(2)}, u32[]{:S(2)}) %all-to-all-start) | async-done | bytes 288 | tf_op jit(solution)/shard_map/all_to_all | solution.py:100
  327.6 64.2 %reduce-scatter.5.cloned.1.call-done = f32[128,4096]{1,0:T(8,128)} async-done(((f32[512,4096]{1,0:T(8,128)}), f32[128,4096]{1,0:T(8,128)}) %reduce-scatter.5.cloned.1.call-update) | async-done | bytes 2097168 | tf_op jit(solution)/shard_map/reduce_scatter | solution.py:73
  391.9 2.6 fusion.7
  394.5 0.2 copy.50
  394.7 1.4 copy.57
  396.2 3.4 gather_fusion
  399.6 3.2 broadcast_select_fusion
  402.7 7.4 %all-to-all-start.3 = ((bf16[32,2,128,128]{3,2,1,0:T(8,128)(2,1)}), bf16[32,2,128,128]{3,2,1,0:T(8,128)(2,1)}, u32[]{:S(2)}, u32[]{:S(2)}) async-start(bf16[32,2,128,128]{3,2,1,0:T(8,128)(2,1)} %broadcast_select_fusion), calls=%async_computation.5 | async-start | bytes 4194304 | tf_op jit(solution)/shard_map/all_to_all | solution.py:103
  410.1 29.9 %all-to-all-done.3 = bf16[32,2,128,128]{3,2,1,0:T(8,128)(2,1)} async-done(((bf16[32,2,128,128]{3,2,1,0:T(8,128)(2,1)}), bf16[32,2,128,128]{3,2,1,0:T(8,128)(2,1)}, u32[]{:S(2)}, u32[]{:S(2)}) %all-to-all-start.3) | async-done | bytes 2097184 | tf_op jit(solution)/shard_map/all_to_all | solution.py:103
  440.1 3.3 gather_fusion.1
  443.3 1.4 select_bitcast_fusion
  444.8 6.9 %fusion.4 = f32[32,1,3,1]{2,1,3,0:T(1,128)S(1)} fusion(bf16[32,3,128,128]{3,2,1,0:T(8,128)(2,1)S(1)} %copy-done, bf16[32,128,128,1]{2,1,0,3:T(8,128)(2,1)S(1)} %select_bitcast_fusion), kind=kOutput, calls=%fused_computation.6 | convolution fusion | flops 3145728 | bytes 4194688 | tf_op jit(solution)/shard_map/eij,exij->xe/dot_general | solution.py:105
  451.7 0.8 convolution_multiply_fusion
  (41 shorter events, 1.7 us)
Async XLA Ops:
  6.5 438.2 %copy-start = (bf16[32,3,128,128]{3,2,1,0:T(8,128)(2,1)S(1)}, bf16[32,3,128,128]{3,2,1,0:T(8,128)(2,1)}, u32[]{:S(2)}) copy-start(bf16[32,3,128,128]{3,2,1,0:T(8,128)(2,1)} %param.11) | copy-start | bytes 9437188
  6.5 117.5 %all-gather.6.cloned.1.call-start = ((), (), s32[]{:S(2)}) async-start(), calls=%async_computation.9 | async-start | bytes 17825792 | tf_op jit(solution)/shard_map/all_gather | solution.py:50
  9.9 209.4 %reduce-scatter.3.cloned.1.call-start = ((), (), s32[]{:S(2)}) async-start(), calls=%async_computation.6 | async-start | bytes 10485760 | tf_op jit(solution)/shard_map/reduce_scatter | solution.py:68
  139.2 131.0 %all-gather.4.cloned.1.call-start = ((), (), s32[]{:S(2)}) async-start(), calls=%async_computation.7 | async-start | bytes 5242880 | tf_op jit(solution)/shard_map/all_gather | solution.py:71
  222.1 169.8 %reduce-scatter.5.cloned.1.call-start = ((), (), s32[]{:S(2)}) async-start(), calls=%async_computation.8 | async-start | bytes 10485760 | tf_op jit(solution)/shard_map/reduce_scatter | solution.py:73
  310.8 0.7 copy-start.1
  310.8 1.0 copy-start.2
  312.6 14.6 %all-to-all-start = ((s32[32,1,2]{2,1,0:T(1,128)}), s32[32,1,2]{2,1,0:T(1,128)S(1)}, u32[]{:S(2)}, u32[]{:S(2)}) async-start(s32[32,1,2]{2,1,0:T(1,128)} %bitcast.3), calls=%async_computation | async-start | bytes 32768 | tf_op jit(solution)/shard_map/all_to_all | solution.py:100
  402.7 37.4 %all-to-all-start.3 = ((bf16[32,2,128,128]{3,2,1,0:T(8,128)(2,1)}), bf16[32,2,128,128]{3,2,1,0:T(8,128)(2,1)}, u32[]{:S(2)}, u32[]{:S(2)}) async-start(bf16[32,2,128,128]{3,2,1,0:T(8,128)(2,1)} %broadcast_select_fusion), calls=%async_computation.5 | async-start | bytes 4194304 | tf_op jit(solution)/shard_map/all_to_all | solution.py:103
  444.7 6.9 %copy-start.3 = (s32[32]{0:T(128)S(1)}, s32[32]{0:T(128)}, u32[]{:S(2)}) copy-start(s32[32]{0:T(128)} %param.10) | copy-start | bytes 388
Sparse Core Ops, SparseCore 0:
  10.0 113.9 all-gather.5
  139.3 80.0 reduce-scatter.2
  222.2 47.9 all-gather.3
  311.0 80.8 reduce-scatter.4
where the time goes:
time: 460 us; the launch traced here: 459 us
  waiting for transfers between devices  329 us (72%)
  local copies, waits for them, and re-layouts  37.8 us (8%)
  matrix products  37.4 us (8%)
  starting transfers between devices  14.8 us (3%)
  other arithmetic  14.8 us (3%)
  between operations  13.3 us (3%)
  blocking collectives  11.8 us (3%)
    all_gather x1, waiting for transfers between devices, multiply(): row_strip = lax.all_gather(right_part, 'row', axis=0, tiled=True)  99.4 us
    reduce_scatter x1, waiting for transfers between devices, shards(): lax.psum_scatter(partial_square, 'layer', scatter_dimension=0, tiled=True)  80.1 us
    reduce_scatter x1, waiting for transfers between devices, shards(): lax.psum_scatter(partial_cube, 'layer', scatter_dimension=0, tiled=True)  64.2 us
    all_gather x1, waiting for transfers between devices, shards(): square = lax.all_gather(square_share, 'layer', axis=0, tiled=True)  48.1 us
    all_to_all x1, waiting for transfers between devices, shards(): lax.all_to_all(fetched, ('row', 'col'), split_axis=0, concat_axis=0, tile...  29.9 us
    dot_general x2, matrix products, multiply(): jnp.dot(gathered_copies(left_part, 'col', 1), row_strip, preferred_elemen...  29.7 us
    unnamed x13, local copies, waits for them, and re-layouts  13.3 us
    all_to_all x2, blocking collectives, copy_for_each(): lax.all_to_all(jnp.broadcast_to(value[None], (length, *value.shape)), axi...  11.8 us
  transfers between devices with their start and end apart: 6, of which 6 were waited for; matrix products, arithmetic and copies ran while one was open for 2% of the time, Pallas kernels for 0%

commit v1 on v0

--- a/solution.py
+++ b/solution.py
@@ -2,6 +2,7 @@
 import jax.numpy as jnp
 from jax import lax
 from jax.sharding import PartitionSpec as P
+from jax.lax import axis_index, axis_size, ppermute
 
 BS = 128
 ATOM_DEV = 8
@@ -47,7 +48,28 @@
 def multiply(left_matrix, right_matrix, layer_count, layer_id):
     left_part = column_subset(left_matrix, layer_count, layer_id)
     right_part = row_subset(right_matrix, layer_count, layer_id)
-    row_strip = lax.all_gather(right_part, "row", axis=0, tiled=True)
+    y_new = axis_index("row")
+    heard = axis_size("row")
+    spare, x_next, out_arr = (heard, y_new, right_part.shape[0])
+    so_far_all = [s * spare if i == 0 else s for i, s in enumerate(right_part.shape)]
+    wide_out = passed = right_part
+    row_strip = lax.dynamic_update_slice_in_dim(
+        jnp.zeros(so_far_all, right_part.dtype), right_part, x_next * out_arr, axis=0
+    )
+    for num in tuple(range(1, spare // 2 + 1)):
+        wide_out = ppermute(
+            wide_out, axis_name="row", perm=[(i, (i + 1) % spare) for i in range(spare)]
+        )
+        row_strip = lax.dynamic_update_slice_in_dim(
+            row_strip, wide_out, (x_next - num) % spare * out_arr, axis=0
+        )
+        if 2 * num < spare:
+            passed = ppermute(
+                passed, axis_name="row", perm=[(i, (i - 1) % spare) for i in range(spare)]
+            )
+            row_strip = lax.dynamic_update_slice_in_dim(
+                row_strip, passed, (x_next + num) % spare * out_arr, axis=0
+            )
     return jnp.dot(
         gathered_copies(left_part, "col", 1), row_strip, preferred_element_type=jnp.float32
     )

time: 460 us -> 560 us (1.22)
  starting transfers between devices: 14.8 us -> 60.3 us
  local copies, waits for them, and re-layouts: 37.8 us -> 70 us
  waiting for transfers between devices: 329 us -> 357 us
  blocking collectives: 11.8 us -> 5.42 us
    ppermute x0 -> x15, waiting for transfers between devices: none -> 130 us  [the longest x8 79.3 us: multiply(): ppermute(wide_out, axis_name='row', perm=[(i, (i + 1) % spare) for i in r...]
    all_gather x1 -> x0, waiting for transfers between devices: 99.4 us -> none  [multiply(): row_strip = lax.all_gather(right_part, 'row', axis=0, tiled=True)]
    ppermute x0 -> x15, starting transfers between devices: none -> 40.4 us  [the longest x7 38.8 us: multiply(): ppermute(passed, axis_name='row', perm=[(i, (i - 1) % spare) for i in ran...]
    dynamic_update_slice x0 -> x15, local copies, waits for them, and re-layouts: none -> 24.7 us  [the longest x8 13.6 us: multiply(): lax.dynamic_update_slice_in_dim(row_strip, wide_out, (x_next - num) % spa...]
    all_to_all x2 -> x1, blocking collectives: 11.8 us -> 5.42 us  [copy_for_each(): lax.all_to_all(jnp.broadcast_to(value[None], (length, *value.shape)), axi...]
    another operation x0 -> x1, local copies, waits for them, and re-layouts: none -> 5.97 us
    unnamed x13 -> x17, local copies, waits for them, and re-layouts: 13.3 us -> 13.7 us
  transfers between devices with their start and end apart: 6 -> 21, of which waited for: 6 -> 17; matrix products, arithmetic and copies ran while one was open for 2% -> 6% of each run, Pallas kernels for 0% -> 0%
where the time goes in v1:
time: 560 us; the launch traced here: 559 us
  waiting for transfers between devices  357 us (64%)
  local copies, waits for them, and re-layouts  70 us (12%)
  starting transfers between devices  60.3 us (11%)
  matrix products  37.4 us (7%)
  other arithmetic  14.9 us (3%)
  between operations  13.6 us (2%)
    ppermute x8, waiting for transfers between devices, multiply(): ppermute(wide_out, axis_name='row', perm=[(i, (i + 1) % spare) for i in r...  79.3 us
    reduce_scatter x1, waiting for transfers between devices, shards(): lax.psum_scatter(partial_square, 'layer', scatter_dimension=0, tiled=True)  76.8 us
    reduce_scatter x1, waiting for transfers between devices, shards(): lax.psum_scatter(partial_cube, 'layer', scatter_dimension=0, tiled=True)  64.6 us
    ppermute x7, waiting for transfers between devices, multiply(): ppermute(passed, axis_name='row', perm=[(i, (i - 1) % spare) for i in ran...  51.1 us
    all_gather x1, waiting for transfers between devices, shards(): square = lax.all_gather(square_share, 'layer', axis=0, tiled=True)  48.1 us
    ppermute x7, starting transfers between devices, multiply(): ppermute(passed, axis_name='row', perm=[(i, (i - 1) % spare) for i in ran...  38.8 us
    all_to_all x1, waiting for transfers between devices, shards(): lax.all_to_all(fetched, ('row', 'col'), split_axis=0, concat_axis=0, tile...  29.9 us
    dot_general x2, matrix products, multiply(): jnp.dot(gathered_copies(left_part, 'col', 1), row_strip, preferred_elemen...  29.7 us
  transfers between devices with their start and end apart: 21, of which 17 were waited for; matrix products, arithmetic and copies ran while one was open for 6% of the time, Pallas kernels for 0%

profile of v1, /device:TPU:0, one launch (start us, length us, event | category | flops | bytes accessed | tf_op | source)
XLA Modules:
  0.0 558.6 jit_solution(14970949051798907830)
XLA Ops:
  7.6 6.0 %broadcast.104 = bf16[2048,4096]{1,0:T(8,128)(2,1)} broadcast(bf16[]{:T(256)} %constant.189.clone.1), dimensions={} | broadcast | bytes 16777218 | tf_op jit(solution)/shard_map/broadcast.3
  17.6 4.9 collective-permute-start.1
  22.5 23.2 %collective-permute-done = bf16[128,4096]{1,0:T(8,128)(2,1)S(1)} collective-permute-done((bf16[128,4096]{1,0:T(8,128)(2,1)S(1)}, bf16[128,4096]{1,0:T(8,128)(2,1)S(1)}, u32[]{:S(2)}, u32[]{:S(2)}) %collective-permute-start) | collective-permute-done | bytes 1048608 | tf_op jit(solution)/shard_map/ppermute | solution.py:60
  46.7 5.3 collective-permute-start.3
  52.0 21.4 %collective-permute-done.2 = bf16[128,4096]{1,0:T(8,128)(2,1)} collective-permute-done((bf16[128,4096]{1,0:T(8,128)(2,1)S(1)}, bf16[128,4096]{1,0:T(8,128)(2,1)}, u32[]{:S(2)}, u32[]{:S(2)}) %collective-permute-start.2) | collective-permute-done | bytes 1048608 | tf_op jit(solution)/shard_map/ppermute | solution.py:60
  73.6 5.9 %collective-permute-start.5 = (bf16[128,4096]{1,0:T(8,128)(2,1)}, bf16[128,4096]{1,0:T(8,128)(2,1)}, u32[]{:S(2)}, u32[]{:S(2)}) collective-permute-start(bf16[128,4096]{1,0:T(8,128)(2,1)} %collective-permute-done.3), channel_id=1, source_target_pairs={{0,30},{2,0},{4,2},{6,4},{8,6},{10,8},{12,10},{14,12},{16,14},{18,... | collective-permute-start | bytes 3145736 | tf_op jit(solution)/shard_map/ppermute | solution.py:67
  79.6 6.5 %copy.40 = bf16[512,4096]{0,1:T(8,128)(2,1)} copy(bf16[512,4096]{1,0:T(8,128)(2,1)} %param.6) | data formatting | bytes 8388608 | tf_op args[0]
  86.3 14.2 %collective-permute-done.4 = bf16[128,4096]{1,0:T(8,128)(2,1)} collective-permute-done((bf16[128,4096]{1,0:T(8,128)(2,1)}, bf16[128,4096]{1,0:T(8,128)(2,1)}, u32[]{:S(2)}, u32[]{:S(2)}) %collective-permute-start.4) | collective-permute-done | bytes 1048608 | tf_op jit(solution)/shard_map/ppermute | solution.py:60
  110.7 5.4 collective-permute-start.7
  118.4 8.3 %collective-permute-done.6 = bf16[128,4096]{1,0:T(8,128)(2,1)} collective-permute-done((bf16[128,4096]{1,0:T(8,128)(2,1)}, bf16[128,4096]{1,0:T(8,128)(2,1)}, u32[]{:S(2)}, u32[]{:S(2)}) %collective-permute-start.6) | collective-permute-done | bytes 1048608 | tf_op jit(solution)/shard_map/ppermute | solution.py:60
  131.3 7.9 %collective-permute-done.7 = bf16[128,4096]{1,0:T(8,128)(2,1)S(1)} collective-permute-done((bf16[128,4096]{1,0:T(8,128)(2,1)}, bf16[128,4096]{1,0:T(8,128)(2,1)S(1)}, u32[]{:S(2)}, u32[]{:S(2)}) %collective-permute-start.7) | collective-permute-done | bytes 1048608 | tf_op jit(solution)/shard_map/ppermute | solution.py:67
  139.2 5.7 %collective-permute-start.9 = (bf16[128,4096]{1,0:T(8,128)(2,1)S(1)}, bf16[128,4096]{1,0:T(8,128)(2,1)S(1)}, u32[]{:S(2)}, u32[]{:S(2)}) collective-permute-start(bf16[128,4096]{1,0:T(8,128)(2,1)S(1)} %collective-permute-done.7), channel_id=1, source_target_pairs={{0,30},{2,0},{4,2},{6,4},{8,6},{10,8},{12,10},{14,12},{16,14},{18,... | collective-permute-start | bytes 3145736 | tf_op jit(solution)/shard_map/ppermute | solution.py:67
  156.4 10.4 %collective-permute-done.9 = bf16[128,4096]{1,0:T(8,128)(2,1)S(1)} collective-permute-done((bf16[128,4096]{1,0:T(8,128)(2,1)S(1)}, bf16[128,4096]{1,0:T(8,128)(2,1)S(1)}, u32[]{:S(2)}, u32[]{:S(2)}) %collective-permute-start.9) | collective-permute-done | bytes 1048608 | tf_op jit(solution)/shard_map/ppermute | solution.py:67
  166.8 5.8 %collective-permute-start.11 = (bf16[128,4096]{1,0:T(8,128)(2,1)S(1)}, bf16[128,4096]{1,0:T(8,128)(2,1)S(1)}, u32[]{:S(2)}, u32[]{:S(2)}) collective-permute-start(bf16[128,4096]{1,0:T(8,128)(2,1)S(1)} %collective-permute-done.9), channel_id=1, source_target_pairs={{0,30},{2,0},{4,2},{6,4},{8,6},{10,8},{12,10},{14,12},{16,14},{18,... | collective-permute-start | bytes 3145736 | tf_op jit(solution)/shard_map/ppermute | solution.py:67
  177.9 15.7 %collective-permute-done.11 = bf16[128,4096]{1,0:T(8,128)(2,1)S(1)} collective-permute-done((bf16[128,4096]{1,0:T(8,128)(2,1)S(1)}, bf16[128,4096]{1,0:T(8,128)(2,1)S(1)}, u32[]{:S(2)}, u32[]{:S(2)}) %collective-permute-start.11) | collective-permute-done | bytes 1048608 | tf_op jit(solution)/shard_map/ppermute | solution.py:67
  193.6 5.8 %collective-permute-start.13 = (bf16[128,4096]{1,0:T(8,128)(2,1)S(1)}, bf16[128,4096]{1,0:T(8,128)(2,1)S(1)}, u32[]{:S(2)}, u32[]{:S(2)}) collective-permute-start(bf16[128,4096]{1,0:T(8,128)(2,1)S(1)} %collective-permute-done.11), channel_id=1, source_target_pairs={{0,30},{2,0},{4,2},{6,4},{8,6},{10,8},{12,10},{14,12},{16,14},{18,... | collective-permute-start | bytes 3145736 | tf_op jit(solution)/shard_map/ppermute | solution.py:67
  202.5 16.9 %collective-permute-done.13 = bf16[128,4096]{1,0:T(8,128)(2,1)S(1)} collective-permute-done((bf16[128,4096]{1,0:T(8,128)(2,1)S(1)}, bf16[128,4096]{1,0:T(8,128)(2,1)S(1)}, u32[]{:S(2)}, u32[]{:S(2)}) %collective-permute-start.13) | collective-permute-done | bytes 1048608 | tf_op jit(solution)/shard_map/ppermute | solution.py:67
  220.6 5.4 collective-permute-done.14
  227.1 15.1 %fusion.9 = f32[512,4096]{1,0:T(8,128)} fusion(bf16[512,2048]{0,1:T(8,128)(2,1)} %bitcast.10, bf16[2048,4096]{1,0:T(8,128)(2,1)} %constant_dynamic-update-slice_fusion), kind=kOutput, calls=%fused_computation.57 | convolution fusion | flops 8589934592 | bytes 27262976 | tf_op jit(solution)/shard_map/dot_general | solution.py:73
  242.4 76.8 %reduce-scatter.3.cloned.1.call-done = f32[128,4096]{1,0:T(8,128)} async-done(((f32[512,4096]{1,0:T(8,128)}), f32[128,4096]{1,0:T(8,128)}) %reduce-scatter.3.cloned.1.call-update) | async-done | bytes 2097168 | tf_op jit(solution)/shard_map/reduce_scatter | solution.py:90
  322.0 48.1 %all-gather.2.cloned.1.call-done = bf16[512,4096]{1,0:T(8,128)(2,1)} async-done(((bf16[128,4096]{1,0:T(8,128)(2,1)}), bf16[512,4096]{1,0:T(8,128)(2,1)}) %all-gather.2.cloned.1.call-update) | async-done | bytes 4194320 | tf_op jit(solution)/shard_map/all_gather | solution.py:93
  370.1 7.7 %reshape.121 = bf16[512,8,4,128]{3,2,1,0:T(4,128)(2,1)} reshape(bf16[512,4096]{1,0:T(8,128)(2,1)} %all-gather.2.cloned.1.call-done) | data formatting | bytes 8388608 | tf_op jit(solution)/shard_map/reshape | solution.py:37
  377.8 5.6 %constant_dynamic-slice_fusion = bf16[512,8,1,128]{3,2,1,0:T(2,128)(2,1)} fusion(bf16[512,8,4,128]{3,2,1,0:T(4,128)(2,1)} %reshape.121, s32[]{:T(128)S(6)} %select_n.225), kind=kLoop, calls=%fused_computation.24 | loop fusion | bytes 2097156 | tf_op jit(solution)/shard_map/jit(dynamic_index_in_dim)/dynamic_slice | solution.py:38
  383.4 5.8 %copy.48 = bf16[512,8,1,128]{0,3,1,2:T(8,128)(2,1)} copy(bf16[512,8,1,128]{3,2,1,0:T(2,128)(2,1)} %constant_dynamic-slice_fusion) | data formatting | bytes 2097152
  390.6 5.4 all_to_all.30
  396.1 14.6 %fusion.10 = f32[512,4096]{1,0:T(8,128)} fusion(bf16[512,2048]{0,1:T(8,128)(2,1)S(1)} %bitcast.69, bf16[2048,4096]{1,0:T(8,128)(2,1)} %constant_dynamic-update-slice_fusion), kind=kOutput, calls=%fused_computation.58 | convolution fusion | flops 8589934592 | bytes 27262976 | tf_op jit(solution)/shard_map/dot_general | solution.py:73
  411.8 7.5 %all-to-all-start = ((s32[32,1,2]{2,1,0:T(1,128)}), s32[32,1,2]{2,1,0:T(1,128)S(1)}, u32[]{:S(2)}, u32[]{:S(2)}) async-start(s32[32,1,2]{2,1,0:T(1,128)} %bitcast.3), calls=%async_computation | async-start | bytes 32768 | tf_op jit(solution)/shard_map/all_to_all | solution.py:122
  419.4 7.3 %all-to-all-done = s32[32,1,2]{2,1,0:T(1,128)S(1)} async-done(((s32[32,1,2]{2,1,0:T(1,128)}), s32[32,1,2]{2,1,0:T(1,128)S(1)}, u32[]{:S(2)}, u32[]{:S(2)}) %all-to-all-start) | async-done | bytes 288 | tf_op jit(solution)/shard_map/all_to_all | solution.py:122
  427.0 64.6 %reduce-scatter.5.cloned.1.call-done = f32[128,4096]{1,0:T(8,128)} async-done(((f32[512,4096]{1,0:T(8,128)}), f32[128,4096]{1,0:T(8,128)}) %reduce-scatter.5.cloned.1.call-update) | async-done | bytes 2097168 | tf_op jit(solution)/shard_map/reduce_scatter | solution.py:95
  502.4 7.4 %all-to-all-start.3 = ((bf16[32,2,128,128]{3,2,1,0:T(8,128)(2,1)}), bf16[32,2,128,128]{3,2,1,0:T(8,128)(2,1)}, u32[]{:S(2)}, u32[]{:S(2)}) async-start(bf16[32,2,128,128]{3,2,1,0:T(8,128)(2,1)} %broadcast_select_fusion), calls=%async_computation.5 | async-start | bytes 4194304 | tf_op jit(solution)/shard_map/all_to_all | solution.py:125
  509.8 29.9 %all-to-all-done.3 = bf16[32,2,128,128]{3,2,1,0:T(8,128)(2,1)} async-done(((bf16[32,2,128,128]{3,2,1,0:T(8,128)(2,1)}), bf16[32,2,128,128]{3,2,1,0:T(8,128)(2,1)}, u32[]{:S(2)}, u32[]{:S(2)}) %all-to-all-start.3) | async-done | bytes 2097184 | tf_op jit(solution)/shard_map/all_to_all | solution.py:125
  544.4 6.9 %fusion = f32[32,1,3,1]{2,1,3,0:T(1,128)S(1)} fusion(bf16[32,3,128,128]{3,2,1,0:T(8,128)(2,1)S(1)} %copy-done, bf16[32,128,128,1]{2,1,0,3:T(8,128)(2,1)S(1)} %select_bitcast_fusion), kind=kOutput, calls=%fused_computation.2 | convolution fusion | flops 3145728 | bytes 4194688 | tf_op jit(solution)/shard_map/eij,exij->xe/dot_general | solution.py:127
  (89 shorter events, 67.5 us)
Async XLA Ops:
  6.5 537.9 %copy-start = (bf16[32,3,128,128]{3,2,1,0:T(8,128)(2,1)S(1)}, bf16[32,3,128,128]{3,2,1,0:T(8,128)(2,1)}, u32[]{:S(2)}) copy-start(bf16[32,3,128,128]{3,2,1,0:T(8,128)(2,1)} %param.11) | copy-start | bytes 9437188
  16.0 29.7 %collective-permute-start = (bf16[128,4096]{1,0:T(8,128)(2,1)S(1)}, bf16[128,4096]{1,0:T(8,128)(2,1)S(1)}, u32[]{:S(2)}, u32[]{:S(2)}) collective-permute-start(bf16[128,4096]{1,0:T(8,128)(2,1)S(1)} %get-tuple-element.8), channel_id=1, source_target_pairs={{0,2},{2,4},{4,6},{6,8},{8,10},{10,12},{12,14},{14,16},{16,18},{18... | collective-permute-start | bytes 3145736 | tf_op jit(solution)/shard_map/ppermute | solution.py:60
  17.6 28.1 %collective-permute-start.1 = (bf16[128,4096]{1,0:T(8,128)(2,1)S(1)}, bf16[128,4096]{1,0:T(8,128)(2,1)S(1)}, u32[]{:S(2)}, u32[]{:S(2)}) collective-permute-start(bf16[128,4096]{1,0:T(8,128)(2,1)S(1)} %get-tuple-element.8), channel_id=1, source_target_pairs={{0,30},{2,0},{4,2},{6,4},{8,6},{10,8},{12,10},{14,12},{16,14},{18,... | collective-permute-start | bytes 3145736 | tf_op jit(solution)/shard_map/ppermute | solution.py:67
  45.7 27.9 %copy-start.2 = (bf16[128,4096]{1,0:T(8,128)(2,1)}, bf16[128,4096]{1,0:T(8,128)(2,1)S(1)}, u32[]{:S(2)}) copy-start(bf16[128,4096]{1,0:T(8,128)(2,1)S(1)} %collective-permute-done) | copy-start | bytes 3145732
  45.7 27.8 %collective-permute-start.2 = (bf16[128,4096]{1,0:T(8,128)(2,1)S(1)}, bf16[128,4096]{1,0:T(8,128)(2,1)}, u32[]{:S(2)}, u32[]{:S(2)}) collective-permute-start(bf16[128,4096]{1,0:T(8,128)(2,1)S(1)} %collective-permute-done), channel_id=1, source_target_pairs={{0,2},{2,4},{4,6},{6,8},{8,10},{10,12},{12,14},{14,16},{16,18},{18... | collective-permute-start | bytes 3145736 | tf_op jit(solution)/shard_map/ppermute | solution.py:60
  45.7 1.0 copy-start.1
  46.7 26.9 %collective-permute-start.3 = (bf16[128,4096]{1,0:T(8,128)(2,1)S(1)}, bf16[128,4096]{1,0:T(8,128)(2,1)}, u32[]{:S(2)}, u32[]{:S(2)}) collective-permute-start(bf16[128,4096]{1,0:T(8,128)(2,1)S(1)} %collective-permute-done.1), channel_id=1, source_target_pairs={{0,30},{2,0},{4,2},{6,4},{8,6},{10,8},{12,10},{14,12},{16,14},{18,... | collective-permute-start | bytes 3145736 | tf_op jit(solution)/shard_map/ppermute | solution.py:67
  73.4 27.1 %collective-permute-start.4 = (bf16[128,4096]{1,0:T(8,128)(2,1)}, bf16[128,4096]{1,0:T(8,128)(2,1)}, u32[]{:S(2)}, u32[]{:S(2)}) collective-permute-start(bf16[128,4096]{1,0:T(8,128)(2,1)} %collective-permute-done.2), channel_id=1, source_target_pairs={{0,2},{2,4},{4,6},{6,8},{8,10},{10,12},{12,14},{14,16},{16,18},{18... | collective-permute-start | bytes 3145736 | tf_op jit(solution)/shard_map/ppermute | solution.py:60
  73.6 37.1 %collective-permute-start.5 = (bf16[128,4096]{1,0:T(8,128)(2,1)}, bf16[128,4096]{1,0:T(8,128)(2,1)}, u32[]{:S(2)}, u32[]{:S(2)}) collective-permute-start(bf16[128,4096]{1,0:T(8,128)(2,1)} %collective-permute-done.3), channel_id=1, source_target_pairs={{0,30},{2,0},{4,2},{6,4},{8,6},{10,8},{12,10},{14,12},{16,14},{18,... | collective-permute-start | bytes 3145736 | tf_op jit(solution)/shard_map/ppermute | solution.py:67
  100.5 26.1 %collective-permute-start.6 = (bf16[128,4096]{1,0:T(8,128)(2,1)}, bf16[128,4096]{1,0:T(8,128)(2,1)}, u32[]{:S(2)}, u32[]{:S(2)}) collective-permute-start(bf16[128,4096]{1,0:T(8,128)(2,1)} %collective-permute-done.4), channel_id=1, source_target_pairs={{0,2},{2,4},{4,6},{6,8},{8,10},{10,12},{12,14},{14,16},{16,18},{18... | collective-permute-start | bytes 3145736 | tf_op jit(solution)/shard_map/ppermute | solution.py:60
  103.3 123.9 %all-to-all-start.1 = ((bf16[2,512,1024]{1,2,0:T(8,128)(2,1)}), bf16[2,512,1024]{1,2,0:T(8,128)(2,1)}, u32[]{:S(2)}, u32[]{:S(2)}) async-start(bf16[2,512,1024]{1,2,0:T(8,128)(2,1)} %broadcast_in_dim.109), calls=%async_computation.1 | async-start | bytes 4194304 | tf_op jit(solution)/shard_map/all_to_all | solution.py:19
  108.1 211.1 %reduce-scatter.3.cloned.1.call-start = ((), (), s32[]{:S(2)}) async-start(), calls=%async_computation.6 | async-start | bytes 10485760 | tf_op jit(solution)/shard_map/reduce_scatter | solution.py:90
  110.7 28.4 %collective-permute-start.7 = (bf16[128,4096]{1,0:T(8,128)(2,1)}, bf16[128,4096]{1,0:T(8,128)(2,1)S(1)}, u32[]{:S(2)}, u32[]{:S(2)}) collective-permute-start(bf16[128,4096]{1,0:T(8,128)(2,1)} %collective-permute-done.5), channel_id=1, source_target_pairs={{0,30},{2,0},{4,2},{6,4},{8,6},{10,8},{12,10},{14,12},{16,14},{18,... | collective-permute-start | bytes 3145736 | tf_op jit(solution)/shard_map/ppermute | solution.py:67
  126.6 25.1 %collective-permute-start.8 = (bf16[128,4096]{1,0:T(8,128)(2,1)}, bf16[128,4096]{1,0:T(8,128)(2,1)S(1)}, u32[]{:S(2)}, u32[]{:S(2)}) collective-permute-start(bf16[128,4096]{1,0:T(8,128)(2,1)} %collective-permute-done.6), channel_id=1, source_target_pairs={{0,2},{2,4},{4,6},{6,8},{8,10},{10,12},{12,14},{14,16},{16,18},{18... | collective-permute-start | bytes 3145736 | tf_op jit(solution)/shard_map/ppermute | solution.py:60
  139.2 27.6 %collective-permute-start.9 = (bf16[128,4096]{1,0:T(8,128)(2,1)S(1)}, bf16[128,4096]{1,0:T(8,128)(2,1)S(1)}, u32[]{:S(2)}, u32[]{:S(2)}) collective-permute-start(bf16[128,4096]{1,0:T(8,128)(2,1)S(1)} %collective-permute-done.7), channel_id=1, source_target_pairs={{0,30},{2,0},{4,2},{6,4},{8,6},{10,8},{12,10},{14,12},{16,14},{18,... | collective-permute-start | bytes 3145736 | tf_op jit(solution)/shard_map/ppermute | solution.py:67
  151.8 24.0 %collective-permute-start.10 = (bf16[128,4096]{1,0:T(8,128)(2,1)S(1)}, bf16[128,4096]{1,0:T(8,128)(2,1)S(1)}, u32[]{:S(2)}, u32[]{:S(2)}) collective-permute-start(bf16[128,4096]{1,0:T(8,128)(2,1)S(1)} %collective-permute-done.8), channel_id=1, source_target_pairs={{0,2},{2,4},{4,6},{6,8},{8,10},{10,12},{12,14},{14,16},{16,18},{18... | collective-permute-start | bytes 3145736 | tf_op jit(solution)/shard_map/ppermute | solution.py:60
  166.8 26.8 %collective-permute-start.11 = (bf16[128,4096]{1,0:T(8,128)(2,1)S(1)}, bf16[128,4096]{1,0:T(8,128)(2,1)S(1)}, u32[]{:S(2)}, u32[]{:S(2)}) collective-permute-start(bf16[128,4096]{1,0:T(8,128)(2,1)S(1)} %collective-permute-done.9), channel_id=1, source_target_pairs={{0,30},{2,0},{4,2},{6,4},{8,6},{10,8},{12,10},{14,12},{16,14},{18,... | collective-permute-start | bytes 3145736 | tf_op jit(solution)/shard_map/ppermute | solution.py:67
  175.7 24.7 %collective-permute-start.12 = (bf16[128,4096]{1,0:T(8,128)(2,1)S(1)}, bf16[128,4096]{1,0:T(8,128)(2,1)S(1)}, u32[]{:S(2)}, u32[]{:S(2)}) collective-permute-start(bf16[128,4096]{1,0:T(8,128)(2,1)S(1)} %collective-permute-done.10), channel_id=1, source_target_pairs={{0,2},{2,4},{4,6},{6,8},{8,10},{10,12},{12,14},{14,16},{16,18},{18... | collective-permute-start | bytes 3145736 | tf_op jit(solution)/shard_map/ppermute | solution.py:60
  193.6 25.9 %collective-permute-start.13 = (bf16[128,4096]{1,0:T(8,128)(2,1)S(1)}, bf16[128,4096]{1,0:T(8,128)(2,1)S(1)}, u32[]{:S(2)}, u32[]{:S(2)}) collective-permute-start(bf16[128,4096]{1,0:T(8,128)(2,1)S(1)} %collective-permute-done.11), channel_id=1, source_target_pairs={{0,30},{2,0},{4,2},{6,4},{8,6},{10,8},{12,10},{14,12},{16,14},{18,... | collective-permute-start | bytes 3145736 | tf_op jit(solution)/shard_map/ppermute | solution.py:67
  200.4 25.6 %collective-permute-start.14 = (bf16[128,4096]{1,0:T(8,128)(2,1)S(1)}, bf16[128,4096]{1,0:T(8,128)(2,1)S(1)}, u32[]{:S(2)}, u32[]{:S(2)}) collective-permute-start(bf16[128,4096]{1,0:T(8,128)(2,1)S(1)} %collective-permute-done.12), channel_id=1, source_target_pairs={{0,2},{2,4},{4,6},{6,8},{8,10},{10,12},{12,14},{14,16},{16,18},{18... | collective-permute-start | bytes 3145736 | tf_op jit(solution)/shard_map/ppermute | solution.py:60
  242.3 127.7 %all-gather.2.cloned.1.call-start = ((), (), s32[]{:S(2)}) async-start(), calls=%async_computation.7 | async-start | bytes 5242880 | tf_op jit(solution)/shard_map/all_gather | solution.py:93
  321.9 169.7 %reduce-scatter.5.cloned.1.call-start = ((), (), s32[]{:S(2)}) async-start(), calls=%async_computation.8 | async-start | bytes 10485760 | tf_op jit(solution)/shard_map/reduce_scatter | solution.py:95
  396.1 14.6 %copy-start.3 = (s32[32,1]{0,1:T(1,128)S(1)}, s32[32,1]{0,1:T(1,128)}, u32[]{:S(2)}) copy-start(s32[32,1]{0,1:T(1,128)} %param.8) | copy-start | bytes 388
  396.1 14.9 %copy-start.4 = (s32[32]{0:T(128)S(1)}, s32[32]{0:T(128)}, u32[]{:S(2)}) copy-start(s32[32]{0:T(128)} %param.9) | copy-start | bytes 388
  411.8 14.8 %all-to-all-start = ((s32[32,1,2]{2,1,0:T(1,128)}), s32[32,1,2]{2,1,0:T(1,128)S(1)}, u32[]{:S(2)}, u32[]{:S(2)}) async-start(s32[32,1,2]{2,1,0:T(1,128)} %bitcast.3), calls=%async_computation | async-start | bytes 32768 | tf_op jit(solution)/shard_map/all_to_all | solution.py:122
  502.4 37.4 %all-to-all-start.3 = ((bf16[32,2,128,128]{3,2,1,0:T(8,128)(2,1)}), bf16[32,2,128,128]{3,2,1,0:T(8,128)(2,1)}, u32[]{:S(2)}, u32[]{:S(2)}) async-start(bf16[32,2,128,128]{3,2,1,0:T(8,128)(2,1)} %broadcast_select_fusion), calls=%async_computation.5 | async-start | bytes 4194304 | tf_op jit(solution)/shard_map/all_to_all | solution.py:125
  544.4 6.9 %copy-start.5 = (s32[32]{0:T(128)S(1)}, s32[32]{0:T(128)}, u32[]{:S(2)}) copy-start(s32[32]{0:T(128)} %param.10) | copy-start | bytes 388
Sparse Core Ops, SparseCore 0:
  242.4 76.7 reduce-scatter.2
  322.0 47.9 all-gather.1
  410.8 80.8 reduce-scatter.4
